TPU v7x, 256 devices: a whole 4x4x8 slice. The times are simulated.
256 devices in a mesh: lon: 16 (over z, x_hi), lat: 16 (over y, x_lo, core).
Axes of the slice: x: 4 (x_hi: 2, x_lo: 2; x = x_hi * 2 + x_lo), y: 4, z: 8, core: 2. Of those that a mesh axis runs over, the one named last changes fastest.
Arguments:
- tracers: float32 [2, 8, 2048, 4096], P(None, None, 'lat', 'lon'), may hold values from -6 to 6
- zonal_vel: float32 [8, 2048, 4096], P(None, 'lat', 'lon'), may hold values from -3 to 3
- merid_vel: float32 [8, 2048, 4096], P(None, 'lat', 'lon'), may hold values from -3 to 3
- thickness: float32 [8, 2048, 4096], P(None, 'lat', 'lon'), may hold values from 0.5 to 2
- land_sea: int32 [8, 2048, 4096], P(None, 'lat', 'lon'), may hold values from 0 to 1, as said below
- cell_dx: float32 [2048, 4096], P('lat', 'lon'), may hold values from 0.5 to 1.5
- cell_dy: float32 [2048, 4096], P('lat', 'lon'), may hold values from 0.5 to 1.5
- fold_partner: int32 [4096], P('lon'), may hold values from 0 to 4095, as said below
Outputs:
- new_tracers: float32 [2, 8, 2048, 4096], P(None, None, 'lat', 'lon')
Inputs may be any that keep to these rules, and one draw needn't show every extreme that they name: In each column the ocean cells are the top levels: land_sea is 1 on levels above a column depth of 1 to 8 levels and 0 below it. fold_partner[i] = (4095 - i + p) mod 4096 with one pivot p of 1 to 255 for all i.
All inputs are finite; a program needn't handle non-finite values.
Results may differ from a plain program's by a relative error of at most 0.00002.
Values sent between devices are 32-bit elements; how exact they have to be, the bound alone decides.
No kernel may reach another device: no remote copies, remote signals or barrier semaphores. Data moves between devices by JAX's collectives and lax.ppermute only.
A program may use at most 128 MiB of HBM per device.

v0:
```python
import jax
import jax.numpy as jnp
from jax import lax
from jax.sharding import PartitionSpec as P

TIME_STEP = 0.2
DIFFUSIVITY = 0.25


def extended(array, sides, width, wrap):
    for axis, dim in sides:
        count, length = (lax.axis_size(axis), array.shape[dim])
        up = [(i, (i + 1) % count) for i in range(count if wrap else count - 1)]
        down = [(j, i) for i, j in up]
        last = lax.slice_in_dim(array, length - width, length, axis=dim)
        leading = lax.slice_in_dim(array, 0, width, axis=dim)
        before = lax.ppermute(last, axis, up)
        after = lax.ppermute(leading, axis, down)
        array = jnp.concatenate([before, array, after], axis=dim)
    return array


def from_behind(array, axis, by):
    count = lax.axis_size(axis)
    return lax.ppermute(array, axis, [(i, (i + by) % count) for i in range(count)])


def shifted(value, axis, steps):
    count = lax.axis_size(axis)
    leading, last = (max(0, -steps), min(count, count - steps))
    return lax.ppermute(value, axis, [(source, source + steps) for source in range(leading, last)])


def tendency(
    trac_lon,
    trac_lat,
    thick_lon,
    thick_lat,
    dx_lon,
    dx_lat,
    dy_lon,
    dy_lat,
    u_faces,
    v_faces,
    volume,
):
    dy_u = 0.5 * (dy_lon[:, :-1] + dy_lon[:, 1:])
    dx_u = 0.5 * (dx_lon[:, :-1] + dx_lon[:, 1:])
    thick_u = jnp.minimum(thick_lon[..., :-1], thick_lon[..., 1:])
    trans_u = u_faces * dy_u * thick_u
    diff_u = DIFFUSIVITY * dy_u * thick_u / dx_u
    flux_x = trans_u * 0.5 * (trac_lon[..., :-1] + trac_lon[..., 1:]) - diff_u * (
        trac_lon[..., 1:] - trac_lon[..., :-1]
    )
    dx_v = 0.5 * (dx_lat[:-1, :] + dx_lat[1:, :])
    dy_v = 0.5 * (dy_lat[:-1, :] + dy_lat[1:, :])
    thick_v = jnp.minimum(thick_lat[..., :-1, :], thick_lat[..., 1:, :])
    trans_v = v_faces * dx_v * thick_v
    diff_v = DIFFUSIVITY * dx_v * thick_v / dy_v
    flux_y = trans_v * 0.5 * (trac_lat[..., :-1, :] + trac_lat[..., 1:, :]) - diff_v * (
        trac_lat[..., 1:, :] - trac_lat[..., :-1, :]
    )
    divergence = flux_x[..., 1:] - flux_x[..., :-1] + (flux_y[..., 1:, :] - flux_y[..., :-1, :])
    return -divergence / volume


def partner_window(top_rows, fold_partner):
    cycle_size = lax.axis_size("lon")
    cols_here = top_rows.shape[2]
    total = cycle_size * cols_here
    wanted = jnp.concatenate(
        [(fold_partner[:1] + 1) % total, fold_partner, (fold_partner[-1:] - 1 + total) % total]
    )
    gathered = lax.all_gather(top_rows, "lon", axis=2, tiled=True)
    return jnp.take(gathered, wanted, axis=2)


def extend(stack, fold_partner):
    lon_side = extended(stack, (("lon", 2),), 1, True)
    lat_side = extended(stack, (("lat", 1),), 1, False)
    ghost_row = partner_window(stack[:, -1:, :], fold_partner)[:, 0, 1:-1]
    at_top = lax.axis_index("lat") == lax.axis_size("lat") - 1
    upper_row = jnp.where(at_top, ghost_row, lat_side[:, -1, :])
    lat_side = jnp.concatenate([lat_side[:, :-1, :], upper_row[:, None, :]], axis=1)
    return (lon_side, lat_side)


def section_by_section(
    tracers, zonal_vel, merid_vel, thickness, sea_mask, wet_thick, cell_dx, cell_dy, fold_partner
):
    levels = thickness.shape[0]
    rows_here = thickness.shape[1]
    cols_here = thickness.shape[2]
    volume = cell_dx * cell_dy * thickness
    geometry = jnp.concatenate([wet_thick, cell_dx[None], cell_dy[None]], axis=0)
    flat_tracers = tracers.reshape(2 * levels, rows_here, cols_here)
    west_u = from_behind(zonal_vel[:, :, -1:], "lon", 1)
    u_faces = jnp.concatenate([west_u, zonal_vel], axis=2)
    south_v = shifted(merid_vel[:, -1:, :], "lat", 1)
    v_faces = jnp.concatenate([south_v, merid_vel], axis=1)
    geo_lon, geo_lat = extend(geometry, fold_partner)
    trac_lon, trac_lat = extend(flat_tracers, fold_partner)

    def operator(field_lon, field_lat):
        return tendency(
            field_lon.reshape(2, levels, rows_here, cols_here + 2),
            field_lat.reshape(2, levels, rows_here + 2, cols_here),
            geo_lon[:levels],
            geo_lat[:levels],
            geo_lon[levels],
            geo_lat[levels],
            geo_lon[levels + 1],
            geo_lat[levels + 1],
            u_faces,
            v_faces,
            volume,
        )

    first = operator(trac_lon, trac_lat)
    section = tracers + TIME_STEP * first
    section_lon, section_lat = extend(
        section.reshape(2 * levels, rows_here, cols_here), fold_partner
    )
    second = operator(section_lon, section_lat)
    return sea_mask * (tracers + 0.5 * TIME_STEP * (first + second))


def shards(tracers, zonal_vel, merid_vel, thickness, land_sea, cell_dx, cell_dy, fold_partner):
    sea_mask = land_sea.astype(jnp.float32)
    wet_thick = thickness * sea_mask
    return section_by_section(
        tracers,
        zonal_vel,
        merid_vel,
        thickness,
        sea_mask,
        wet_thick,
        cell_dx,
        cell_dy,
        fold_partner,
    )


def solution(mesh):
    return jax.shard_map(
        shards,
        mesh=mesh,
        in_specs=(
            P(None, None, "lat", "lon"),
            P(None, "lat", "lon"),
            P(None, "lat", "lon"),
            P(None, "lat", "lon"),
            P(None, "lat", "lon"),
            P("lat", "lon"),
            P("lat", "lon"),
            P("lon"),
        ),
        out_specs=P(None, None, "lat", "lon"),
        check_vma=False,
    )
```

profile of v0, /device:TPU:116, one launch (start us, length us, event | category | flops | bytes accessed | tf_op | source)
XLA Modules:
  0.0 362.2 jit_solution(13244162745184583832)
XLA Ops:
  0.0 1.0 mul.221
  1.0 2.8 convert_multiply_fusion
  3.8 1.2 pad_maximum_fusion.8
  5.0 3.0 copy.218
  8.0 1.4 fusion.28
  9.4 3.1 collective-permute-start.1
  13.0 2.5 copy.216
  15.5 1.3 slice.243
  16.8 5.2 %collective-permute-start = (f32[8,128,1]{1,0,2:T(8,128)}, f32[8,128,1]{1,0,2:T(8,128)}, u32[]{:S(2)}, u32[]{:S(2)}) collective-permute-start(f32[8,128,1]{1,0,2:T(8,128)} %slice.243), channel_id=1, source_target_pairs={{0,16},{16,32},{32,48},{48,64},{64,80},{80,96},{96,112},{112,128},... | collective-permute-start | bytes 12296 | tf_op jit(solution)/shard_map/ppermute | solution.py:25
  22.0 1.5 fusion.29
  23.5 0.8 copy.251
  24.3 1.9 collective-permute-start.6
  26.8 0.8 copy.253
  27.6 4.1 %collective-permute-start.8 = (f32[16,1,256]{0,2,1:T(8,128)S(1)}, f32[16,1,256]{0,2,1:T(8,128)}, u32[]{:S(2)}, u32[]{:S(2)}) collective-permute-start(f32[16,1,256]{0,2,1:T(8,128)S(1)} %copy.253), channel_id=1, source_target_pairs={{0,1},{1,2},{2,3},{3,4},{4,5},{5,6},{6,7},{7,8},{8,9},{9,10},{10,1... | collective-permute-start | bytes 49160 | tf_op jit(solution)/shard_map/ppermute | solution.py:17
  31.8 1.6 fusion.26
  35.2 70.0 %all_gather.10 = f32[16,1,4096]{0,2,1:T(8,128)} all-gather(f32[16,1,256]{0,2,1:T(8,128)S(1)} %copy.253), channel_id=1, replica_groups=mesh['lon'=16,'lat'=16] {'lon'}, dimensions={2}, use_global_device_ids=true | all-gather | bytes 278528 | tf_op jit(solution)/shard_map/all_gather | solution.py:74
  105.2 1.6 constant_dynamic-update-slice_fusion
  108.7 72.2 %all_gather.9 = f32[10,1,4096]{0,2,1:T(8,128)} all-gather(f32[10,1,256]{0,2,1:T(8,128)} %copy.251), channel_id=1, replica_groups=mesh['lon'=16,'lat'=16] {'lon'}, dimensions={2}, use_global_device_ids=true | all-gather | bytes 174080 | tf_op jit(solution)/shard_map/all_gather | solution.py:74
  180.9 2.9 copy.222
  183.8 2.3 convert_element_type.3
  186.0 2.1 copy.226
  188.2 2.1 copy.228
  190.3 1.3 slice.255
  191.6 1.5 copy.252
  193.0 1.4 slice.211
  195.2 3.3 gather_fusion
  198.5 3.3 gather_fusion.1
  201.9 3.5 collective-permute-start.4
  205.4 1.0 maximum_bitcast_fusion
  207.8 1.9 collective-permute-start.7
  209.8 2.9 fusion.14
  212.7 2.9 copy.225
  215.6 2.9 copy.230
  218.5 2.4 collective-permute-start.5
  220.9 1.3 copy.227
  222.2 4.2 %collective-permute-start.9 = (f32[16,1,256]{0,2,1:T(8,128)}, f32[16,1,256]{0,2,1:T(8,128)}, u32[]{:S(2)}, u32[]{:S(2)}) collective-permute-start(f32[16,1,256]{0,2,1:T(8,128)} %copy.254), channel_id=1, source_target_pairs={{1,0},{2,1},{3,2},{4,3},{5,4},{6,5},{7,6},{8,7},{9,8},{10,9},{11,1... | collective-permute-start | bytes 49160 | tf_op jit(solution)/shard_map/ppermute | solution.py:18
  226.5 1.3 copy.229
  227.8 5.1 %multiply_subtract_fusion.1 = f32[2,8,128,257]{3,2,1,0:T(8,128)} fusion(f32[2,8,128,1]{3,2,1,0:T(8,128)} %copy.229, f32[2,8,128,256]{3,2,1,0:T(8,128)S(1)} %copy-done, f32[2,8,128,1]{3,2,1,0:T(8,128)} %copy.227, f32[8,128,257]{2,1,0:T(8,128)} %copy.230, f32[8,128,257]{2,1,0:T(8,128)} %copy.225), kind=kLoop, calls=%fused_computation.8 | loop fusion | flops 3684352 | bytes 6324224 | tf_op jit(solution)/shard_map/sub | solution.py:52
  233.0 1.7 fusion.21
  234.6 1.0 copy.234
  235.6 1.6 copy.232
  238.0 1.0 maximum_maximum_fusion
  239.2 2.4 fusion.11
  241.6 1.0 fusion.20
  242.8 1.0 copy.236
  243.8 1.6 dynamic-update-slice.1
  245.4 2.9 multiply_subtract_fusion.3
  248.9 2.2 multiply_add_fusion
  251.1 1.9 fusion.24
  253.2 1.6 copy.241
  254.7 2.2 collective-permute-start.10
  257.0 2.1 copy.243
  259.1 1.3 collective-permute-start.11
  260.5 71.2 %all_gather.11 = f32[16,1,4096]{0,2,1:T(8,128)} all-gather(f32[16,1,256]{0,2,1:T(8,128)S(1)} %copy.255), channel_id=1, replica_groups=mesh['lon'=16,'lat'=16] {'lon'}, dimensions={2}, use_global_device_ids=true | all-gather | bytes 278528 | tf_op jit(solution)/shard_map/all_gather | solution.py:74
  331.8 1.9 collective-permute-start.12
  333.7 2.6 gather_fusion.2
  337.1 4.5 %collective-permute-start.13 = (f32[16,1,256]{0,2,1:T(8,128)}, f32[16,1,256]{0,2,1:T(8,128)S(1)}, u32[]{:S(2)}, u32[]{:S(2)}) collective-permute-start(f32[16,1,256]{0,2,1:T(8,128)} %copy.256), channel_id=1, source_target_pairs={{1,0},{2,1},{3,2},{4,3},{5,4},{6,5},{7,6},{8,7},{9,8},{10,9},{11,1... | collective-permute-start | bytes 49160 | tf_op jit(solution)/shard_map/ppermute | solution.py:18
  341.6 2.1 copy.242
  343.8 2.0 copy.244
  345.8 6.3 %multiply_subtract_fusion = f32[2,8,128,257]{3,2,1,0:T(8,128)} fusion(f32[2,8,128,1]{3,2,1,0:T(8,128)} %copy.244, f32[2,8,128,256]{3,2,1,0:T(8,128)} %copy-done.1, f32[2,8,128,1]{3,2,1,0:T(8,128)} %copy.242, f32[8,128,257]{2,1,0:T(8,128)} %copy.230, f32[8,128,257]{2,1,0:T(8,128)} %copy.225), kind=kLoop, calls=%fused_computation.7 | loop fusion | flops 3684352 | bytes 6324224 | tf_op jit(solution)/shard_map/sub | solution.py:52
  352.8 1.0 fusion.19
  353.9 1.0 copy.246
  354.9 3.5 multiply_subtract_fusion.2
  359.6 2.6 fusion.9
  (71 shorter events, 10.3 us)
Async XLA Ops:
  1.0 2.8 copy-start.8
  1.0 2.8 copy-start.9
  5.0 21.2 %copy-start = (f32[2,8,128,256]{3,2,1,0:T(8,128)S(1)}, f32[2,8,128,256]{3,2,1,0:T(8,128)}, u32[]{:S(2)}) copy-start(f32[2,8,128,256]{3,2,1,0:T(8,128)} %param.10) | copy-start | bytes 6291460
  9.4 192.4 %collective-permute-start.1 = (f32[10,128,1]{1,2,0:T(1,128)}, f32[10,128,1]{1,2,0:T(1,128)}, u32[]{:S(2)}, u32[]{:S(2)}) collective-permute-start(f32[10,128,1]{1,2,0:T(1,128)} %get-tuple-element.27), channel_id=1, source_target_pairs={{0,16},{16,32},{32,48},{48,64},{64,80},{80,96},{96,112},{112,128},... | collective-permute-start | bytes 15368 | tf_op jit(solution)/shard_map/ppermute | solution.py:17
  12.5 189.4 %collective-permute-start.2 = (f32[10,128,1]{1,2,0:T(1,128)}, f32[10,128,1]{1,2,0:T(1,128)}, u32[]{:S(2)}, u32[]{:S(2)}) collective-permute-start(f32[10,128,1]{1,2,0:T(1,128)} %get-tuple-element.28), channel_id=1, source_target_pairs={{16,0},{32,16},{48,32},{64,48},{80,64},{96,80},{112,96},{128,112},... | collective-permute-start | bytes 15368 | tf_op jit(solution)/shard_map/ppermute | solution.py:18
  16.8 191.1 %collective-permute-start = (f32[8,128,1]{1,0,2:T(8,128)}, f32[8,128,1]{1,0,2:T(8,128)}, u32[]{:S(2)}, u32[]{:S(2)}) collective-permute-start(f32[8,128,1]{1,0,2:T(8,128)} %slice.243), channel_id=1, source_target_pairs={{0,16},{16,32},{32,48},{48,64},{64,80},{80,96},{96,112},{112,128},... | collective-permute-start | bytes 12296 | tf_op jit(solution)/shard_map/ppermute | solution.py:25
  24.3 211.3 %collective-permute-start.6 = (f32[10,1,256]{0,2,1:T(8,128)}, f32[10,1,256]{0,2,1:T(8,128)}, u32[]{:S(2)}, u32[]{:S(2)}) collective-permute-start(f32[10,1,256]{0,2,1:T(8,128)} %copy.251), channel_id=1, source_target_pairs={{0,1},{1,2},{2,3},{3,4},{4,5},{5,6},{6,7},{7,8},{8,9},{9,10},{10,1... | collective-permute-start | bytes 30728 | tf_op jit(solution)/shard_map/ppermute | solution.py:17
  27.6 5.8 %copy-start.15 = (s32[256]{0:T(256)S(1)}, s32[256]{0:T(256)}, u32[]{:S(2)}) copy-start(s32[256]{0:T(256)} %param.17) | copy-start | bytes 3076
  27.6 215.1 %collective-permute-start.8 = (f32[16,1,256]{0,2,1:T(8,128)S(1)}, f32[16,1,256]{0,2,1:T(8,128)}, u32[]{:S(2)}, u32[]{:S(2)}) collective-permute-start(f32[16,1,256]{0,2,1:T(8,128)S(1)} %copy.253), channel_id=1, source_target_pairs={{0,1},{1,2},{2,3},{3,4},{4,5},{5,6},{6,7},{7,8},{8,9},{9,10},{10,1... | collective-permute-start | bytes 49160 | tf_op jit(solution)/shard_map/ppermute | solution.py:17
  201.9 7.9 %copy-start.5 = (f32[10,128,256]{1,0,2:T(8,128)S(1)}, f32[10,128,256]{1,0,2:T(8,128)}, u32[]{:S(2)}) copy-start(f32[10,128,256]{1,0,2:T(8,128)} %copy.222) | copy-start | bytes 3932164
  201.9 16.6 %collective-permute-start.3 = (f32[16,128,1]{1,0,2:T(8,128)}, f32[16,128,1]{1,0,2:T(8,128)S(1)}, u32[]{:S(2)}, u32[]{:S(2)}) collective-permute-start(f32[16,128,1]{1,0,2:T(8,128)} %copy.226), channel_id=1, source_target_pairs={{0,16},{16,32},{32,48},{48,64},{64,80},{80,96},{96,112},{112,128},... | collective-permute-start | bytes 24584 | tf_op jit(solution)/shard_map/ppermute | solution.py:17
  201.9 20.4 %collective-permute-start.4 = (f32[16,128,1]{1,0,2:T(8,128)}, f32[16,128,1]{1,0,2:T(8,128)S(1)}, u32[]{:S(2)}, u32[]{:S(2)}) collective-permute-start(f32[16,128,1]{1,0,2:T(8,128)} %copy.228), channel_id=1, source_target_pairs={{16,0},{32,16},{48,32},{64,48},{80,64},{96,80},{112,96},{128,112},... | collective-permute-start | bytes 24584 | tf_op jit(solution)/shard_map/ppermute | solution.py:18
  207.8 25.1 %collective-permute-start.7 = (f32[10,1,256]{0,2,1:T(8,128)}, f32[10,1,256]{0,2,1:T(8,128)}, u32[]{:S(2)}, u32[]{:S(2)}) collective-permute-start(f32[10,1,256]{0,2,1:T(8,128)} %copy.252), channel_id=1, source_target_pairs={{1,0},{2,1},{3,2},{4,3},{5,4},{6,5},{7,6},{8,7},{9,8},{10,9},{11,1... | collective-permute-start | bytes 30728 | tf_op jit(solution)/shard_map/ppermute | solution.py:18
  218.5 20.5 %collective-permute-start.5 = (f32[8,1,256]{2,1,0:T(1,128)}, f32[8,1,256]{2,1,0:T(1,128)}, u32[]{:S(2)}, u32[]{:S(2)}) collective-permute-start(f32[8,1,256]{2,1,0:T(1,128)} %slice.211), channel_id=1, source_target_pairs={{0,1},{1,2},{2,3},{3,4},{4,5},{5,6},{6,7},{7,8},{8,9},{9,10},{10,1... | collective-permute-start | bytes 24584 | tf_op jit(solution)/shard_map/ppermute | solution.py:31
  222.2 19.4 %collective-permute-start.9 = (f32[16,1,256]{0,2,1:T(8,128)}, f32[16,1,256]{0,2,1:T(8,128)}, u32[]{:S(2)}, u32[]{:S(2)}) collective-permute-start(f32[16,1,256]{0,2,1:T(8,128)} %copy.254), channel_id=1, source_target_pairs={{1,0},{2,1},{3,2},{4,3},{5,4},{6,5},{7,6},{8,7},{9,8},{10,9},{11,1... | collective-permute-start | bytes 49160 | tf_op jit(solution)/shard_map/ppermute | solution.py:18
  227.8 5.1 %copy-start.12 = (f32[258,10]{1,0:T(8,128)S(1)}, f32[258,10]{1,0:T(8,128)}, u32[]{:S(2)}) copy-start(f32[258,10]{1,0:T(8,128)} %gather_fusion) | copy-start | bytes 30964
  227.8 5.1 %copy-start.16 = (pred[256]{0:T(512)(128)(4,1)S(1)}, pred[256]{0:T(512)(128)(4,1)}, u32[]{:S(2)}) copy-start(pred[256]{0:T(512)(128)(4,1)} %slice.255) | copy-start | bytes 772
  238.0 1.2 copy-start.10
  239.2 2.4 copy-start.11
  245.4 3.2 copy-start.2
  245.4 3.5 copy-start.4
  251.1 2.0 copy-start.1
  253.1 80.6 %copy-start.14 = (s32[1024]{0:T(1024)S(1)}, s32[1024]{0:T(1024)}, u32[]{:S(2)}) copy-start(s32[1024]{0:T(1024)} %pad_clamp_fusion) | copy-start | bytes 12292
  254.7 86.9 %collective-permute-start.10 = (f32[16,128,1]{1,0,2:T(8,128)S(1)}, f32[16,128,1]{1,0,2:T(8,128)}, u32[]{:S(2)}, u32[]{:S(2)}) collective-permute-start(f32[16,128,1]{1,0,2:T(8,128)S(1)} %copy.241), channel_id=1, source_target_pairs={{0,16},{16,32},{32,48},{48,64},{64,80},{80,96},{96,112},{112,128},... | collective-permute-start | bytes 24584 | tf_op jit(solution)/shard_map/ppermute | solution.py:17
  259.1 84.7 %collective-permute-start.11 = (f32[16,128,1]{1,0,2:T(8,128)}, f32[16,128,1]{1,0,2:T(8,128)}, u32[]{:S(2)}, u32[]{:S(2)}) collective-permute-start(f32[16,128,1]{1,0,2:T(8,128)} %copy.243), channel_id=1, source_target_pairs={{16,0},{32,16},{48,32},{64,48},{80,64},{96,80},{112,96},{128,112},... | collective-permute-start | bytes 24584 | tf_op jit(solution)/shard_map/ppermute | solution.py:18
  331.8 22.1 %collective-permute-start.12 = (f32[16,1,256]{0,2,1:T(8,128)S(1)}, f32[16,1,256]{0,2,1:T(8,128)}, u32[]{:S(2)}, u32[]{:S(2)}) collective-permute-start(f32[16,1,256]{0,2,1:T(8,128)S(1)} %copy.255), channel_id=1, source_target_pairs={{0,1},{1,2},{2,3},{3,4},{4,5},{5,6},{6,7},{7,8},{8,9},{9,10},{10,1... | collective-permute-start | bytes 49160 | tf_op jit(solution)/shard_map/ppermute | solution.py:17
  337.1 15.0 %collective-permute-start.13 = (f32[16,1,256]{0,2,1:T(8,128)}, f32[16,1,256]{0,2,1:T(8,128)S(1)}, u32[]{:S(2)}, u32[]{:S(2)}) collective-permute-start(f32[16,1,256]{0,2,1:T(8,128)} %copy.256), channel_id=1, source_target_pairs={{1,0},{2,1},{3,2},{4,3},{5,4},{6,5},{7,6},{8,7},{9,8},{10,9},{11,1... | collective-permute-start | bytes 49160 | tf_op jit(solution)/shard_map/ppermute | solution.py:18
  352.1 0.7 copy-start.13
  354.9 3.8 %copy-start.3 = (f32[2,8,128,257]{3,2,1,0:T(8,128)S(1)}, f32[2,8,128,257]{3,2,1,0:T(8,128)}, u32[]{:S(2)}) copy-start(f32[2,8,128,257]{3,2,1,0:T(8,128)} %multiply_subtract_fusion) | copy-start | bytes 6316036
  354.9 4.4 %copy-start.6 = (f32[2,8,128,256]{3,2,1,0:T(8,128)S(1)}, f32[2,8,128,256]{3,2,1,0:T(8,128)}, u32[]{:S(2)}) copy-start(f32[2,8,128,256]{3,2,1,0:T(8,128)} %get-tuple-element.7) | copy-start | bytes 6291460
  354.9 4.7 %copy-start.7 = (f32[8,128,256]{2,1,0:T(8,128)S(1)}, f32[8,128,256]{2,1,0:T(8,128)}, u32[]{:S(2)}) copy-start(f32[8,128,256]{2,1,0:T(8,128)} %convert_element_type.3) | copy-start | bytes 3145732
where the time goes:
time: 364 us; the launch traced here: 362 us
  blocking collectives  213 us (59%)
  local copies, waits for them, and re-layouts  66.7 us (18%)
  other arithmetic  43.7 us (12%)
  starting transfers between devices  36.8 us (10%)
    all_gather x3, blocking collectives, partner_window(): gathered = lax.all_gather(top_rows, 'lon', axis=2, tiled=True)  213 us
    ppermute x6, starting transfers between devices, extended(): after = lax.ppermute(leading, axis, down)  16 us
    ppermute x6, starting transfers between devices, extended(): before = lax.ppermute(last, axis, up)  13.2 us
    unnamed x42, local copies, waits for them, and re-layouts  11.5 us
    sub x2, other arithmetic, tendency(): trans_u * 0.5 * (trac_lon[..., :-1] + trac_lon[..., 1:])  11.4 us
    slice x8, local copies, waits for them, and re-layouts, extended(): last = lax.slice_in_dim(array, length - width, length, axis=dim)  10.8 us
    gather x3, local copies, waits for them, and re-layouts, partner_window(): return jnp.take(gathered, wanted, axis=2)  9.24 us
  transfers between devices with their start and end apart: 14, of which 0 were waited for; matrix products, arithmetic and copies ran while one was open for 22% of the time, Pallas kernels for 0%

commit v1 on v0

--- a/solution.py
+++ b/solution.py
@@ -71,7 +71,9 @@
     wanted = jnp.concatenate(
         [(fold_partner[:1] + 1) % total, fold_partner, (fold_partner[-1:] - 1 + total) % total]
     )
-    gathered = lax.all_gather(top_rows, "lon", axis=2, tiled=True)
+    gathered = jnp.concatenate(
+        lax.all_to_all(jnp.stack([top_rows] * lax.axis_size("lon")), "lon", 0, 0), axis=2
+    )
     return jnp.take(gathered, wanted, axis=2)
 
 

time: 364 us -> 184 us (0.51)
  the two profiles are of different devices: /device:TPU:116 before, /device:TPU:8 now
where the time goes in v1:
time: 184 us; the launch traced here: 182 us
  local copies, waits for them, and re-layouts  72.1 us (39%)
  starting transfers between devices  66.1 us (36%)
  other arithmetic  41.5 us (23%)
    all_to_all x3, starting transfers between devices, partner_window(): lax.all_to_all(jnp.stack([top_rows] * lax.axis_size('lon')), 'lon', 0, 0)  25.5 us
    ppermute x6, starting transfers between devices, extended(): after = lax.ppermute(leading, axis, down)  20.9 us
    ppermute x6, starting transfers between devices, extended(): before = lax.ppermute(last, axis, up)  17.4 us
    unnamed x42, local copies, waits for them, and re-layouts  12.4 us
    slice x8, local copies, waits for them, and re-layouts, extended(): last = lax.slice_in_dim(array, length - width, length, axis=dim)  12.2 us
    sub x2, other arithmetic, tendency(): trans_u * 0.5 * (trac_lon[..., :-1] + trac_lon[..., 1:])  11.4 us
    gather x3, local copies, waits for them, and re-layouts, partner_window(): return jnp.take(gathered, wanted, axis=2)  8.42 us
    concatenate x4, local copies, waits for them, and re-layouts, extended(): array = jnp.concatenate([before, array, after], axis=dim)  8.23 us
  transfers between devices with their start and end apart: 17, of which 1 were waited for; matrix products, arithmetic and copies ran while one was open for 48% of the time, Pallas kernels for 0%

profile of v1, /device:TPU:8, one launch (start us, length us, event | category | flops | bytes accessed | tf_op | source)
XLA Modules:
  0.0 182.0 jit_solution(13373167446872437205)
XLA Ops:
  0.0 1.0 mul.221
  1.0 2.7 %convert_multiply_fusion = (f32[8,128,256]{2,1,0:T(8,128)S(1)}, f32[8,128,256]{2,1,0:T(8,128)}) fusion(f32[8,128,256]{2,1,0:T(8,128)} %param.13, s32[8,128,256]{2,1,0:T(8,128)} %param.14, f32[128,256]{1,0:T(8,128)S(1)} %mul.221), kind=kLoop, calls=%fused_computation.76 | loop fusion | flops 786432 | bytes 4325376 | tf_op jit(solution)/shard_map/mul | solution.py:132
  3.7 1.2 pad_maximum_fusion.8
  4.9 3.0 %copy.205 = f32[10,128,256]{1,2,0:T(8,128)} copy(f32[10,128,256]{2,1,0:T(8,128)} %pad_maximum_fusion.8) | data formatting | bytes 2621440 | tf_op jit(solution)/shard_map/concatenate | solution.py:97
  7.9 0.8 fusion.28
  8.7 3.1 %collective-permute-start.1 = (f32[10,128,1]{1,2,0:T(1,128)S(1)}, f32[10,128,1]{1,2,0:T(1,128)S(1)}, u32[]{:S(2)}, u32[]{:S(2)}) collective-permute-start(f32[10,128,1]{1,2,0:T(1,128)S(1)} %get-tuple-element.27), channel_id=1, source_target_pairs={{0,16},{16,32},{32,48},{48,64},{64,80},{80,96},{96,112},{112,128},... | collective-permute-start | bytes 15368 | tf_op jit(solution)/shard_map/ppermute | solution.py:17
  11.8 5.4 %collective-permute-start.2 = (f32[10,128,1]{1,2,0:T(1,128)S(1)}, f32[10,128,1]{1,2,0:T(1,128)S(1)}, u32[]{:S(2)}, u32[]{:S(2)}) collective-permute-start(f32[10,128,1]{1,2,0:T(1,128)S(1)} %get-tuple-element.28), channel_id=1, source_target_pairs={{16,0},{32,16},{48,32},{64,48},{80,64},{96,80},{112,96},{128,112},... | collective-permute-start | bytes 15368 | tf_op jit(solution)/shard_map/ppermute | solution.py:18
  17.2 2.6 %copy.203 = f32[8,128,256]{1,0,2:T(8,128)} copy(f32[8,128,256]{2,1,0:T(8,128)} %param.11) | data formatting | bytes 2097152 | tf_op args[1]
  20.4 1.5 fusion.29
  22.0 1.9 %collective-permute-start.6 = (f32[10,1,256]{2,1,0:T(1,128)}, f32[10,1,256]{2,1,0:T(1,128)}, u32[]{:S(2)}, u32[]{:S(2)}) collective-permute-start(f32[10,1,256]{2,1,0:T(1,128)} %get-tuple-element.31), channel_id=1, source_target_pairs={{0,1},{1,2},{2,3},{3,4},{4,5},{5,6},{6,7},{7,8},{8,9},{9,10},{10,1... | collective-permute-start | bytes 30728 | tf_op jit(solution)/shard_map/ppermute | solution.py:17
  24.6 0.7 stack.6
  25.3 8.8 %all-to-all-start = ((f32[16,10,1,256]{3,2,1,0:T(1,128)}), f32[16,10,1,256]{3,2,1,0:T(1,128)}, u32[]{:S(2)}, u32[]{:S(2)}) async-start(f32[16,10,1,256]{3,2,1,0:T(1,128)} %stack.6), calls=%async_computation | async-start | bytes 327680 | tf_op jit(solution)/shard_map/all_to_all | solution.py:75
  34.8 4.0 %collective-permute-start.8 = (f32[16,1,256]{2,1,0:T(1,128)}, f32[16,1,256]{2,1,0:T(1,128)}, u32[]{:S(2)}, u32[]{:S(2)}) collective-permute-start(f32[16,1,256]{2,1,0:T(1,128)} %get-tuple-element.22), channel_id=1, source_target_pairs={{0,1},{1,2},{2,3},{3,4},{4,5},{5,6},{6,7},{7,8},{8,9},{9,10},{10,1... | collective-permute-start | bytes 49160 | tf_op jit(solution)/shard_map/ppermute | solution.py:17
  38.7 1.7 fusion.26
  42.4 1.5 constant_dynamic-update-slice_fusion
  45.3 2.9 %copy.209 = f32[10,128,256]{1,0,2:T(8,128)} copy(f32[10,128,256]{2,1,0:T(8,128)} %pad_maximum_fusion.8) | data formatting | bytes 2621440 | tf_op jit(solution)/shard_map/concatenate | solution.py:97
  48.9 2.1 %copy.213 = f32[16,128,1]{1,0,2:T(8,128)} copy(f32[16,128,1]{2,1,0:T(8,128)} %get-tuple-element.20) | data formatting | bytes 16384 | tf_op jit(solution)/shard_map/slice | solution.py:15
  51.0 2.1 %copy.215 = f32[16,128,1]{1,0,2:T(8,128)} copy(f32[16,128,1]{2,1,0:T(8,128)} %get-tuple-element.21) | data formatting | bytes 16384 | tf_op jit(solution)/shard_map/slice | solution.py:16
  53.8 0.8 copy.238
  54.6 1.4 slice.217
  56.0 0.7 copy.239
  56.8 3.1 %collective-permute-start.3 = (f32[16,128,1]{1,0,2:T(8,128)}, f32[16,128,1]{1,0,2:T(8,128)}, u32[]{:S(2)}, u32[]{:S(2)}) collective-permute-start(f32[16,128,1]{1,0,2:T(8,128)} %copy.213), channel_id=1, source_target_pairs={{0,16},{16,32},{32,48},{48,64},{64,80},{80,96},{96,112},{112,128},... | collective-permute-start | bytes 24584 | tf_op jit(solution)/shard_map/ppermute | solution.py:17
  59.9 2.5 %collective-permute-start.4 = (f32[16,128,1]{1,0,2:T(8,128)}, f32[16,128,1]{1,0,2:T(8,128)}, u32[]{:S(2)}, u32[]{:S(2)}) collective-permute-start(f32[16,128,1]{1,0,2:T(8,128)} %copy.215), channel_id=1, source_target_pairs={{16,0},{32,16},{48,32},{64,48},{80,64},{96,80},{112,96},{128,112},... | collective-permute-start | bytes 24584 | tf_op jit(solution)/shard_map/ppermute | solution.py:18
  62.4 1.0 maximum_bitcast_fusion
  63.5 2.1 %collective-permute-start.7 = (f32[10,1,256]{0,2,1:T(8,128)}, f32[10,1,256]{0,2,1:T(8,128)S(1)}, u32[]{:S(2)}, u32[]{:S(2)}) collective-permute-start(f32[10,1,256]{0,2,1:T(8,128)} %copy.238), channel_id=1, source_target_pairs={{1,0},{2,1},{3,2},{4,3},{5,4},{6,5},{7,6},{8,7},{9,8},{10,9},{11,1... | collective-permute-start | bytes 30728 | tf_op jit(solution)/shard_map/ppermute | solution.py:18
  65.6 2.9 %fusion.14 = (f32[8,128,257]{1,0,2:T(8,128)}, f32[8,128,257]{1,0,2:T(8,128)}) fusion(f32[8,128,256]{1,0,2:T(8,128)} %copy.203, f32[8,128,1]{1,0,2:T(8,128)} %collective-permute-done, f32[128,257]{0,1:T(8,128)S(1)} %get-tuple-element.35, f32[10,128,1]{1,0,2:T(8,128)S(1)} %copy.211, f32[10,128,256]{1,0,2:T(8,128)S(1)} %copy-done.5, ...), kind=kLoop, calls=%fused_computation.42 | loop fusion | flops 2368512 | bytes 4873728 | tf_op jit(solution)/shard_map/mul | solution.py:52
  68.5 2.9 %copy.212 = f32[8,128,257]{2,1,0:T(8,128)} copy(f32[8,128,257]{1,0,2:T(8,128)} %get-tuple-element.14) | data formatting | bytes 2105344 | tf_op jit(solution)/shard_map/mul | solution.py:52
  71.4 2.8 %copy.217 = f32[8,128,257]{2,1,0:T(8,128)} copy(f32[8,128,257]{1,0,2:T(8,128)} %get-tuple-element.15) | data formatting | bytes 2105344 | tf_op jit(solution)/shard_map/div | solution.py:51
  74.2 2.3 %collective-permute-start.5 = (f32[8,1,256]{2,1,0:T(1,128)}, f32[8,1,256]{2,1,0:T(1,128)}, u32[]{:S(2)}, u32[]{:S(2)}) collective-permute-start(f32[8,1,256]{2,1,0:T(1,128)} %slice.217), channel_id=1, source_target_pairs={{0,1},{1,2},{2,3},{3,4},{4,5},{5,6},{6,7},{7,8},{8,9},{9,10},{10,1... | collective-permute-start | bytes 24584 | tf_op jit(solution)/shard_map/ppermute | solution.py:31
  76.5 2.0 %copy.214 = f32[2,8,128,1]{3,2,1,0:T(8,128)} copy(f32[2,8,128,1]{2,1,0,3:T(8,128)} %bitcast.4) | data formatting | bytes 16384 | tf_op jit(solution)/shard_map/concatenate | solution.py:19
  78.5 4.2 %collective-permute-start.9 = (f32[16,1,256]{0,2,1:T(8,128)}, f32[16,1,256]{0,2,1:T(8,128)}, u32[]{:S(2)}, u32[]{:S(2)}) collective-permute-start(f32[16,1,256]{0,2,1:T(8,128)} %copy.239), channel_id=1, source_target_pairs={{1,0},{2,1},{3,2},{4,3},{5,4},{6,5},{7,6},{8,7},{9,8},{10,9},{11,1... | collective-permute-start | bytes 49160 | tf_op jit(solution)/shard_map/ppermute | solution.py:18
  82.7 2.0 %copy.216 = f32[2,8,128,1]{3,2,1,0:T(8,128)} copy(f32[2,8,128,1]{2,1,0,3:T(8,128)} %bitcast.5) | data formatting | bytes 16384 | tf_op jit(solution)/shard_map/concatenate | solution.py:19
  84.8 5.1 %multiply_subtract_fusion.1 = f32[2,8,128,257]{3,2,1,0:T(8,128)} fusion(f32[2,8,128,1]{3,2,1,0:T(8,128)} %copy.216, f32[2,8,128,256]{3,2,1,0:T(8,128)S(1)} %copy-done, f32[2,8,128,1]{3,2,1,0:T(8,128)} %copy.214, f32[8,128,257]{2,1,0:T(8,128)} %copy.217, f32[8,128,257]{2,1,0:T(8,128)} %copy.212), kind=kLoop, calls=%fused_computation.8 | loop fusion | flops 3684352 | bytes 6324224 | tf_op jit(solution)/shard_map/sub | solution.py:52
  90.6 7.7 %all-to-all-start.1 = ((f32[16,16,1,256]{3,1,2,0:T(8,128)}), f32[16,16,1,256]{3,1,2,0:T(8,128)}, u32[]{:S(2)}, u32[]{:S(2)}) async-start(f32[16,16,1,256]{3,1,2,0:T(8,128)} %stack.7), calls=%async_computation.1 | async-start | bytes 524288 | tf_op jit(solution)/shard_map/all_to_all | solution.py:75
  98.3 2.6 %copy.218 = f32[10,1,16,256]{0,3,2,1:T(8,128)} copy(f32[10,1,16,256]{3,1,0,2:T(1,128)} %bitcast.7) | data formatting | bytes 327680 | tf_op jit(solution)/shard_map/reshape | solution.py:74
  100.9 3.2 %gather_fusion = f32[258,10]{1,0:T(8,128)} fusion(f32[10,4096]{0,1:T(8,128)} %bitcast.57, s32[1024]{0:T(1024)S(1)} %copy-done.13), kind=kCustom, calls=%fused_computation.2 | custom fusion | bytes 21672 | tf_op jit(solution)/shard_map/jit(_take)/gather | solution.py:77
  104.7 1.1 fusion.21
  106.6 1.0 maximum_maximum_fusion
  107.8 2.4 %fusion.11 = (f32[8,129,256]{2,1,0:T(8,128)}, f32[8,129,256]{2,1,0:T(8,128)}) fusion(f32[8,128,256]{2,1,0:T(8,128)S(1)} %copy-done.10, f32[8,1,256]{2,1,0:T(1,128)} %collective-permute-done.5, f32[129,256]{1,0:T(8,128)S(1)} %get-tuple-element.8, f32[10,129,256]{2,1,0:T(8,128)S(1)} %get-tuple-element.30, f32[10,129,256]{2,1,0:T(8,128)S(1)} %get-tuple-element.29, ...), kind=kLoop, calls=%fused_computation.35 | loop fusion | flops 1849344 | bytes 5680128 | tf_op jit(solution)/shard_map/mul | solution.py:60
  110.8 2.9 %copy.222 = f32[16,1,16,256]{0,3,2,1:T(8,128)} copy(f32[16,1,16,256]{3,0,1,2:T(8,128)} %bitcast.16) | data formatting | bytes 524288 | tf_op jit(solution)/shard_map/reshape | solution.py:74
  113.7 2.6 %gather_fusion.1 = f32[258,16]{1,0:T(8,128)S(1)} fusion(f32[16,4096]{0,1:T(8,128)} %bitcast.59, s32[1024]{0:T(1024)S(1)} %copy-done.12), kind=kCustom, calls=%fused_computation.clone | custom fusion | bytes 34056 | tf_op jit(solution)/shard_map/jit(_take)/gather | solution.py:77
  116.3 1.0 fusion.20
  117.5 1.6 dynamic-update-slice.1
  119.1 2.9 %multiply_subtract_fusion.3 = f32[2,8,129,256]{3,2,1,0:T(8,128)S(1)} fusion(f32[2,8,129,256]{3,2,1,0:T(8,128)} %dynamic-update-slice.1, f32[2,8,128,256]{3,2,1,0:T(8,128)S(1)} %copy-done, f32[2,8,1,256]{3,2,1,0:T(1,128)} %bitcast.15, f32[8,129,256]{2,1,0:T(8,128)} %get-tuple-element.13, f32[8,129,256]{2,1,0:T(8,128)} %get-tuple-element.12), kind=kLoop, calls=%fused_computation.13 | loop fusion | flops 3170304 | bytes 8454144 | tf_op jit(solution)/shard_map/sub | solution.py:60
  122.6 2.2 %multiply_add_fusion = (f32[2,8,128,256]{3,2,1,0:T(8,128)S(1)}, f32[2,8,128,256]{3,2,1,0:T(8,128)}) fusion(f32[2,8,128,256]{3,2,1,0:T(8,128)S(1)} %copy-done, f32[8,128,256]{2,1,0:T(8,128)S(1)} %copy-done.4, f32[2,8,129,256]{3,2,1,0:T(8,128)S(1)} %multiply_subtract_fusion.3, f32[2,8,128,257]{3,2,1,0:T(8,128)S(1)} %copy-done.2), kind=kLoop, calls=%fused_computation.27 | loop fusion | flops 3670016 | bytes 15728640 | tf_op jit(solution)/shard_map/add | solution.py:122
  124.9 1.3 copy-done.1
  127.6 0.7 stack.8
  128.3 9.0 %all-to-all-start.2 = ((f32[16,16,1,256]{3,1,2,0:T(8,128)}), f32[16,16,1,256]{3,1,2,0:T(8,128)S(1)}, u32[]{:S(2)}, u32[]{:S(2)}) async-start(f32[16,16,1,256]{3,1,2,0:T(8,128)} %stack.8), calls=%async_computation.2 | async-start | bytes 524288 | tf_op jit(solution)/shard_map/all_to_all | solution.py:75
  137.3 3.2 %fusion.24 = (f32[16,128,1]{2,1,0:T(8,128)}, f32[16,128,1]{2,1,0:T(8,128)}) fusion(f32[16,128,256]{2,1,0:T(8,128)} %bitcast.56), kind=kLoop, calls=%fused_computation.77 | loop fusion | bytes 32768 | tf_op jit(solution)/shard_map/slice | solution.py:15
  140.5 1.6 copy.226
  142.1 3.5 %collective-permute-start.10 = (f32[16,128,1]{1,0,2:T(8,128)S(1)}, f32[16,128,1]{1,0,2:T(8,128)}, u32[]{:S(2)}, u32[]{:S(2)}) collective-permute-start(f32[16,128,1]{1,0,2:T(8,128)S(1)} %copy.226), channel_id=1, source_target_pairs={{0,16},{16,32},{32,48},{48,64},{64,80},{80,96},{96,112},{112,128},... | collective-permute-start | bytes 24584 | tf_op jit(solution)/shard_map/ppermute | solution.py:17
  145.6 2.1 %copy.228 = f32[16,128,1]{1,0,2:T(8,128)} copy(f32[16,128,1]{2,1,0:T(8,128)} %get-tuple-element.17) | data formatting | bytes 16384 | tf_op jit(solution)/shard_map/slice | solution.py:16
  147.7 2.2 %collective-permute-start.11 = (f32[16,128,1]{1,0,2:T(8,128)}, f32[16,128,1]{1,0,2:T(8,128)}, u32[]{:S(2)}, u32[]{:S(2)}) collective-permute-start(f32[16,128,1]{1,0,2:T(8,128)} %copy.228), channel_id=1, source_target_pairs={{16,0},{32,16},{48,32},{64,48},{80,64},{96,80},{112,96},{128,112},... | collective-permute-start | bytes 24584 | tf_op jit(solution)/shard_map/ppermute | solution.py:18
  149.9 2.3 %convert_element_type.3 = f32[8,128,256]{2,1,0:T(8,128)} convert(s32[8,128,256]{2,1,0:T(8,128)} %param.14) | non-fusion elementwise | flops 262144 | bytes 2097152 | tf_op jit(solution)/shard_map/convert_element_type | solution.py:131
  152.2 1.9 %collective-permute-start.12 = (f32[16,1,256]{2,1,0:T(1,128)}, f32[16,1,256]{2,1,0:T(1,128)}, u32[]{:S(2)}, u32[]{:S(2)}) collective-permute-start(f32[16,1,256]{2,1,0:T(1,128)} %get-tuple-element.18), channel_id=1, source_target_pairs={{0,1},{1,2},{2,3},{3,4},{4,5},{5,6},{6,7},{7,8},{8,9},{9,10},{10,1... | collective-permute-start | bytes 49160 | tf_op jit(solution)/shard_map/ppermute | solution.py:17
  154.1 0.8 copy.240
  154.9 4.5 %collective-permute-start.13 = (f32[16,1,256]{0,2,1:T(8,128)}, f32[16,1,256]{0,2,1:T(8,128)S(1)}, u32[]{:S(2)}, u32[]{:S(2)}) collective-permute-start(f32[16,1,256]{0,2,1:T(8,128)} %copy.240), channel_id=1, source_target_pairs={{1,0},{2,1},{3,2},{4,3},{5,4},{6,5},{7,6},{8,7},{9,8},{10,9},{11,1... | collective-permute-start | bytes 49160 | tf_op jit(solution)/shard_map/ppermute | solution.py:18
  159.4 2.1 %copy.227 = f32[2,8,128,1]{3,2,1,0:T(8,128)} copy(f32[2,8,128,1]{2,1,0,3:T(8,128)} %bitcast.25) | data formatting | bytes 16384 | tf_op jit(solution)/shard_map/concatenate | solution.py:19
  161.5 2.0 %copy.229 = f32[2,8,128,1]{3,2,1,0:T(8,128)} copy(f32[2,8,128,1]{2,1,0,3:T(8,128)} %bitcast.26) | data formatting | bytes 16384 | tf_op jit(solution)/shard_map/concatenate | solution.py:19
  163.6 6.3 %multiply_subtract_fusion = f32[2,8,128,257]{3,2,1,0:T(8,128)} fusion(f32[2,8,128,1]{3,2,1,0:T(8,128)} %copy.229, f32[2,8,128,256]{3,2,1,0:T(8,128)} %copy-done.1, f32[2,8,128,1]{3,2,1,0:T(8,128)} %copy.227, f32[8,128,257]{2,1,0:T(8,128)} %copy.217, f32[8,128,257]{2,1,0:T(8,128)} %copy.212), kind=kLoop, calls=%fused_computation.7 | loop fusion | flops 3684352 | bytes 6324224 | tf_op jit(solution)/shard_map/sub | solution.py:52
  169.9 1.9 %copy.231 = f32[16,1,16,256]{0,3,2,1:T(8,128)} copy(f32[16,1,16,256]{3,0,1,2:T(8,128)S(1)} %bitcast.66) | data formatting | bytes 524288 | tf_op jit(solution)/shard_map/reshape | solution.py:74
  171.8 2.6 %gather_fusion.2 = f32[258,16]{1,0:T(8,128)S(1)} fusion(f32[16,4096]{0,1:T(8,128)} %bitcast.58, s32[1024]{0:T(1024)S(1)} %copy-done.12), kind=kCustom, calls=%fused_computation.1.clone | custom fusion | bytes 34056 | tf_op jit(solution)/shard_map/jit(_take)/gather | solution.py:77
  174.7 3.5 %multiply_subtract_fusion.2 = f32[2,8,129,256]{3,2,1,0:T(8,128)S(1)} fusion(f32[2,8,1,256]{3,2,1,0:T(1,128)S(1)} %copy.234, f32[2,8,128,256]{3,2,1,0:T(8,128)} %copy-done.1, f32[2,8,1,256]{3,2,1,0:T(1,128)} %bitcast.27, f32[8,129,256]{2,1,0:T(8,128)} %get-tuple-element.13, f32[8,129,256]{2,1,0:T(8,128)} %get-tuple-element.12), kind=kLoop, calls=%fused_computation.12 | loop fusion | flops 3698688 | bytes 6356992 | tf_op jit(solution)/shard_map/sub | solution.py:60
  179.4 2.6 %fusion.9 = f32[2,8,128,256]{3,2,1,0:T(8,128)} fusion(f32[2,8,128,256]{3,2,1,0:T(8,128)S(1)} %copy-done, f32[2,8,128,256]{3,2,1,0:T(8,128)S(1)} %copy-done.6, f32[2,8,129,256]{3,2,1,0:T(8,128)S(1)} %multiply_subtract_fusion.2, f32[2,8,128,257]{3,2,1,0:T(8,128)S(1)} %copy-done.3, f32[8,128,256]{2,1,0:T(8,128)S(1)} %copy-done.4, f32[8,128,256]{2,1,0:T(8,128)S(1)} %copy-done.7), kind=kLoop, calls=%fused_computation.28 | loop fusion | flops 4718592 | bytes 16777216 | tf_op jit(solution)/shard_map/mul | solution.py:127
  (75 shorter events, 11.8 us)
Async XLA Ops:
  1.0 2.8 %copy-start.8 = (f32[128,256]{1,0:T(8,128)S(1)}, f32[128,256]{1,0:T(8,128)}, u32[]{:S(2)}) copy-start(f32[128,256]{1,0:T(8,128)} %param.15) | copy-start | bytes 393220
  1.0 2.7 %copy-start.9 = (f32[128,256]{1,0:T(8,128)S(1)}, f32[128,256]{1,0:T(8,128)}, u32[]{:S(2)}) copy-start(f32[128,256]{1,0:T(8,128)} %param.16) | copy-start | bytes 393220
  4.9 29.2 %copy-start = (f32[2,8,128,256]{3,2,1,0:T(8,128)S(1)}, f32[2,8,128,256]{3,2,1,0:T(8,128)}, u32[]{:S(2)}) copy-start(f32[2,8,128,256]{3,2,1,0:T(8,128)} %param.10) | copy-start | bytes 6291460
  8.7 48.1 %collective-permute-start.1 = (f32[10,128,1]{1,2,0:T(1,128)S(1)}, f32[10,128,1]{1,2,0:T(1,128)S(1)}, u32[]{:S(2)}, u32[]{:S(2)}) collective-permute-start(f32[10,128,1]{1,2,0:T(1,128)S(1)} %get-tuple-element.27), channel_id=1, source_target_pairs={{0,16},{16,32},{32,48},{48,64},{64,80},{80,96},{96,112},{112,128},... | collective-permute-start | bytes 15368 | tf_op jit(solution)/shard_map/ppermute | solution.py:17
  11.8 48.1 %collective-permute-start.2 = (f32[10,128,1]{1,2,0:T(1,128)S(1)}, f32[10,128,1]{1,2,0:T(1,128)S(1)}, u32[]{:S(2)}, u32[]{:S(2)}) collective-permute-start(f32[10,128,1]{1,2,0:T(1,128)S(1)} %get-tuple-element.28), channel_id=1, source_target_pairs={{16,0},{32,16},{48,32},{64,48},{80,64},{96,80},{112,96},{128,112},... | collective-permute-start | bytes 15368 | tf_op jit(solution)/shard_map/ppermute | solution.py:18
  20.4 43.1 %collective-permute-start = (f32[8,128,1]{1,0,2:T(8,128)S(1)}, f32[8,128,1]{1,0,2:T(8,128)}, u32[]{:S(2)}, u32[]{:S(2)}) collective-permute-start(f32[8,128,1]{1,0,2:T(8,128)S(1)} %slice.252), channel_id=1, source_target_pairs={{0,16},{16,32},{32,48},{48,64},{64,80},{80,96},{96,112},{112,128},... | collective-permute-start | bytes 12296 | tf_op jit(solution)/shard_map/ppermute | solution.py:25
  22.0 83.9 %collective-permute-start.6 = (f32[10,1,256]{2,1,0:T(1,128)}, f32[10,1,256]{2,1,0:T(1,128)}, u32[]{:S(2)}, u32[]{:S(2)}) collective-permute-start(f32[10,1,256]{2,1,0:T(1,128)} %get-tuple-element.31), channel_id=1, source_target_pairs={{0,1},{1,2},{2,3},{3,4},{4,5},{5,6},{6,7},{7,8},{8,9},{9,10},{10,1... | collective-permute-start | bytes 30728 | tf_op jit(solution)/shard_map/ppermute | solution.py:17
  25.3 64.5 %all-to-all-start = ((f32[16,10,1,256]{3,2,1,0:T(1,128)}), f32[16,10,1,256]{3,2,1,0:T(1,128)}, u32[]{:S(2)}, u32[]{:S(2)}) async-start(f32[16,10,1,256]{3,2,1,0:T(1,128)} %stack.6), calls=%async_computation | async-start | bytes 327680 | tf_op jit(solution)/shard_map/all_to_all | solution.py:75
  34.8 5.7 %copy-start.14 = (s32[256]{0:T(256)S(1)}, s32[256]{0:T(256)}, u32[]{:S(2)}) copy-start(s32[256]{0:T(256)} %param.17) | copy-start | bytes 3076
  34.8 84.3 %collective-permute-start.8 = (f32[16,1,256]{2,1,0:T(1,128)}, f32[16,1,256]{2,1,0:T(1,128)}, u32[]{:S(2)}, u32[]{:S(2)}) collective-permute-start(f32[16,1,256]{2,1,0:T(1,128)} %get-tuple-element.22), channel_id=1, source_target_pairs={{0,1},{1,2},{2,3},{3,4},{4,5},{5,6},{6,7},{7,8},{8,9},{9,10},{10,1... | collective-permute-start | bytes 49160 | tf_op jit(solution)/shard_map/ppermute | solution.py:17
  56.8 8.8 %copy-start.5 = (f32[10,128,256]{1,0,2:T(8,128)S(1)}, f32[10,128,256]{1,0,2:T(8,128)}, u32[]{:S(2)}) copy-start(f32[10,128,256]{1,0,2:T(8,128)} %copy.209) | copy-start | bytes 3932164
  56.8 17.5 %collective-permute-start.3 = (f32[16,128,1]{1,0,2:T(8,128)}, f32[16,128,1]{1,0,2:T(8,128)}, u32[]{:S(2)}, u32[]{:S(2)}) collective-permute-start(f32[16,128,1]{1,0,2:T(8,128)} %copy.213), channel_id=1, source_target_pairs={{0,16},{16,32},{32,48},{48,64},{64,80},{80,96},{96,112},{112,128},... | collective-permute-start | bytes 24584 | tf_op jit(solution)/shard_map/ppermute | solution.py:17
  59.9 18.7 %collective-permute-start.4 = (f32[16,128,1]{1,0,2:T(8,128)}, f32[16,128,1]{1,0,2:T(8,128)}, u32[]{:S(2)}, u32[]{:S(2)}) collective-permute-start(f32[16,128,1]{1,0,2:T(8,128)} %copy.215), channel_id=1, source_target_pairs={{16,0},{32,16},{48,32},{64,48},{80,64},{96,80},{112,96},{128,112},... | collective-permute-start | bytes 24584 | tf_op jit(solution)/shard_map/ppermute | solution.py:18
  63.5 40.5 %collective-permute-start.7 = (f32[10,1,256]{0,2,1:T(8,128)}, f32[10,1,256]{0,2,1:T(8,128)S(1)}, u32[]{:S(2)}, u32[]{:S(2)}) collective-permute-start(f32[10,1,256]{0,2,1:T(8,128)} %copy.238), channel_id=1, source_target_pairs={{1,0},{2,1},{3,2},{4,3},{5,4},{6,5},{7,6},{8,7},{9,8},{10,9},{11,1... | collective-permute-start | bytes 30728 | tf_op jit(solution)/shard_map/ppermute | solution.py:18
  74.2 33.4 %collective-permute-start.5 = (f32[8,1,256]{2,1,0:T(1,128)}, f32[8,1,256]{2,1,0:T(1,128)}, u32[]{:S(2)}, u32[]{:S(2)}) collective-permute-start(f32[8,1,256]{2,1,0:T(1,128)} %slice.217), channel_id=1, source_target_pairs={{0,1},{1,2},{2,3},{3,4},{4,5},{5,6},{6,7},{7,8},{8,9},{9,10},{10,1... | collective-permute-start | bytes 24584 | tf_op jit(solution)/shard_map/ppermute | solution.py:31
  78.5 37.8 %collective-permute-start.9 = (f32[16,1,256]{0,2,1:T(8,128)}, f32[16,1,256]{0,2,1:T(8,128)}, u32[]{:S(2)}, u32[]{:S(2)}) collective-permute-start(f32[16,1,256]{0,2,1:T(8,128)} %copy.239), channel_id=1, source_target_pairs={{1,0},{2,1},{3,2},{4,3},{5,4},{6,5},{7,6},{8,7},{9,8},{10,9},{11,1... | collective-permute-start | bytes 49160 | tf_op jit(solution)/shard_map/ppermute | solution.py:18
  90.6 10.3 %copy-start.13 = (s32[1024]{0:T(1024)S(1)}, s32[1024]{0:T(1024)}, u32[]{:S(2)}) copy-start(s32[1024]{0:T(1024)} %pad_clamp_fusion.1) | copy-start | bytes 12292
  90.6 14.1 %copy-start.15 = (pred[256]{0:T(512)(128)(4,1)S(1)}, pred[256]{0:T(512)(128)(4,1)}, u32[]{:S(2)}) copy-start(pred[256]{0:T(512)(128)(4,1)} %slice.264) | copy-start | bytes 772
  90.6 20.2 %all-to-all-start.1 = ((f32[16,16,1,256]{3,1,2,0:T(8,128)}), f32[16,16,1,256]{3,1,2,0:T(8,128)}, u32[]{:S(2)}, u32[]{:S(2)}) async-start(f32[16,16,1,256]{3,1,2,0:T(8,128)} %stack.7), calls=%async_computation.1 | async-start | bytes 524288 | tf_op jit(solution)/shard_map/all_to_all | solution.py:75
  104.0 0.7 copy-start.11
  106.6 1.2 copy-start.10
  110.2 3.4 %copy-start.12 = (s32[1024]{0:T(1024)S(1)}, s32[1024]{0:T(1024)}, u32[]{:S(2)}) copy-start(s32[1024]{0:T(1024)} %pad_clamp_fusion) | copy-start | bytes 12292
  119.1 3.2 %copy-start.2 = (f32[2,8,128,257]{3,2,1,0:T(8,128)S(1)}, f32[2,8,128,257]{3,2,1,0:T(8,128)}, u32[]{:S(2)}) copy-start(f32[2,8,128,257]{3,2,1,0:T(8,128)} %multiply_subtract_fusion.1) | copy-start | bytes 6316036
  119.1 3.5 %copy-start.4 = (f32[8,128,256]{2,1,0:T(8,128)S(1)}, f32[8,128,256]{2,1,0:T(8,128)}, u32[]{:S(2)}) copy-start(f32[8,128,256]{2,1,0:T(8,128)} %get-tuple-element.34) | copy-start | bytes 3145732
  124.9 1.3 copy-start.1
  128.3 41.6 %all-to-all-start.2 = ((f32[16,16,1,256]{3,1,2,0:T(8,128)}), f32[16,16,1,256]{3,1,2,0:T(8,128)S(1)}, u32[]{:S(2)}, u32[]{:S(2)}) async-start(f32[16,16,1,256]{3,1,2,0:T(8,128)} %stack.8), calls=%async_computation.2 | async-start | bytes 524288 | tf_op jit(solution)/shard_map/all_to_all | solution.py:75
  142.1 17.3 %collective-permute-start.10 = (f32[16,128,1]{1,0,2:T(8,128)S(1)}, f32[16,128,1]{1,0,2:T(8,128)}, u32[]{:S(2)}, u32[]{:S(2)}) collective-permute-start(f32[16,128,1]{1,0,2:T(8,128)S(1)} %copy.226), channel_id=1, source_target_pairs={{0,16},{16,32},{32,48},{48,64},{64,80},{80,96},{96,112},{112,128},... | collective-permute-start | bytes 24584 | tf_op jit(solution)/shard_map/ppermute | solution.py:17
  147.7 13.8 %collective-permute-start.11 = (f32[16,128,1]{1,0,2:T(8,128)}, f32[16,128,1]{1,0,2:T(8,128)}, u32[]{:S(2)}, u32[]{:S(2)}) collective-permute-start(f32[16,128,1]{1,0,2:T(8,128)} %copy.228), channel_id=1, source_target_pairs={{16,0},{32,16},{48,32},{64,48},{80,64},{96,80},{112,96},{128,112},... | collective-permute-start | bytes 24584 | tf_op jit(solution)/shard_map/ppermute | solution.py:18
  152.2 22.5 %collective-permute-start.12 = (f32[16,1,256]{2,1,0:T(1,128)}, f32[16,1,256]{2,1,0:T(1,128)}, u32[]{:S(2)}, u32[]{:S(2)}) collective-permute-start(f32[16,1,256]{2,1,0:T(1,128)} %get-tuple-element.18), channel_id=1, source_target_pairs={{0,1},{1,2},{2,3},{3,4},{4,5},{5,6},{6,7},{7,8},{8,9},{9,10},{10,1... | collective-permute-start | bytes 49160 | tf_op jit(solution)/shard_map/ppermute | solution.py:17
  154.9 19.6 %collective-permute-start.13 = (f32[16,1,256]{0,2,1:T(8,128)}, f32[16,1,256]{0,2,1:T(8,128)S(1)}, u32[]{:S(2)}, u32[]{:S(2)}) collective-permute-start(f32[16,1,256]{0,2,1:T(8,128)} %copy.240), channel_id=1, source_target_pairs={{1,0},{2,1},{3,2},{4,3},{5,4},{6,5},{7,6},{8,7},{9,8},{10,9},{11,1... | collective-permute-start | bytes 49160 | tf_op jit(solution)/shard_map/ppermute | solution.py:18
  169.9 4.6 %copy-start.16 = (pred[256]{0:T(512)(128)(4,1)S(1)}, pred[256]{0:T(512)(128)(4,1)}, u32[]{:S(2)}) copy-start(pred[256]{0:T(512)(128)(4,1)} %slice.264) | copy-start | bytes 772
  174.7 3.8 %copy-start.3 = (f32[2,8,128,257]{3,2,1,0:T(8,128)S(1)}, f32[2,8,128,257]{3,2,1,0:T(8,128)}, u32[]{:S(2)}) copy-start(f32[2,8,128,257]{3,2,1,0:T(8,128)} %multiply_subtract_fusion) | copy-start | bytes 6316036
  174.7 4.5 %copy-start.6 = (f32[2,8,128,256]{3,2,1,0:T(8,128)S(1)}, f32[2,8,128,256]{3,2,1,0:T(8,128)}, u32[]{:S(2)}) copy-start(f32[2,8,128,256]{3,2,1,0:T(8,128)} %get-tuple-element.7) | copy-start | bytes 6291460
  174.7 4.7 %copy-start.7 = (f32[8,128,256]{2,1,0:T(8,128)S(1)}, f32[8,128,256]{2,1,0:T(8,128)}, u32[]{:S(2)}) copy-start(f32[8,128,256]{2,1,0:T(8,128)} %convert_element_type.3) | copy-start | bytes 3145732
